TPU v7x, 512 devices: a whole 4x8x8 slice. The times are simulated.
512 devices in a mesh: seq: 16 (over z, core), head: 32 (over x, y).
Axes of the slice: x: 4, y: 8, z: 8, core: 2. Of those that a mesh axis runs over, the one named last changes fastest.
Arguments:
- values: bfloat16 [16384, 8192], P('seq', 'head'), may hold values from -6 to 6
- gate_z: bfloat16 [16384, 8192], P('seq', 'head'), may hold values from -6 to 6
- b_keys: bfloat16 [16384, 8, 128], P('seq'), may hold values from -0.5 to 0.5
- c_queries: bfloat16 [16384, 8, 128], P('seq'), may hold values from -6 to 6
- log_decay: float32 [16384, 128], P('seq', 'head'), may hold values from -2.5 to 0
- level_weight: float32 [16384, 128, 9], P('seq', 'head'), may hold values from 0.2 to 2
- doc_start: int32 [256], replicated, may hold values 0 or 1
- norm_gain: float32 [8192], replicated, may hold values from 0.25 to 1.75
Outputs:
- normed: bfloat16 [16384, 8192], P(('seq', 'head'))
All inputs are finite; a program needn't handle non-finite values.
Results may differ from a plain program's by a relative error of at most 0.0049.
Values may be sent and summed in bfloat16 or wider, within the bound.
A program may use at most 64 MiB of HBM per device.

v0:
```python
import jax
import jax.numpy as jnp
from jax import lax
from jax.experimental import pallas as pl
from jax.experimental.pallas import tpu as pltpu
from jax.sharding import PartitionSpec as P

MESH = pl.DeviceIdType.MESH
F32 = jnp.float32
BF16 = jnp.bfloat16
CHUNK = 128
SPAN = 64
HEADS = 4
DIM = 64
STATE = 128
PER_GROUP = 16
RESET = 128.0


def dot(a, b):
    return jnp.dot(a, b, preferred_element_type=F32)


def kernel(
    n_seq, n_head, b_hbm, c_hbm, v_hbm, g_hbm, decay_hbm, level_hbm, gain_hbm, doc_ref, out_ref,
    pair, wide, keys, query_t, raw, value_t, gate, silu, decay, level, gain,
    ds, tot, key_w, query_w, near, acc, own_state, sib_state, own_decay, all_decay,
    chip_state, chip_states, coef, own_levels, sib_levels, levels, outgoing, arrived,
    load_sem, swap_sem, decay_send, decay_recv, chip_send, chip_recv, rows_send, rows_recv,
):
    me = lax.axis_index("head")
    seq = lax.axis_index("seq")
    z, core = seq // 2, lax.rem(seq, 2)
    n_z = n_seq // 2
    far_levels = n_z.bit_length()
    group = me * HEADS // PER_GROUP
    tokens = v_hbm.shape[0]
    chunks = tokens // CHUNK
    width = HEADS * DIM
    rows_out = tokens // n_head
    per_chunk = CHUNK // rows_out

    loads = [
        pltpu.make_async_copy(decay_hbm, decay, load_sem.at[0]),
        pltpu.make_async_copy(v_hbm, raw, load_sem.at[1]),
        pltpu.make_async_copy(b_hbm.at[:, group // 2], pair.at[0], load_sem.at[2]),
        pltpu.make_async_copy(c_hbm.at[:, group // 2], pair.at[1], load_sem.at[3]),
        pltpu.make_async_copy(level_hbm, level, load_sem.at[4]),
        pltpu.make_async_copy(g_hbm, gate, load_sem.at[5]),
        pltpu.make_async_copy(gain_hbm, gain, load_sem.at[6]),
    ]
    for load in loads:
        load.start()

    barrier = pltpu.get_barrier_semaphore()

    def greet_head(r, _):
        pl.semaphore_signal(
            barrier, inc=1, device_id={"head": lax.rem(me + r, n_head)}, device_id_type=MESH
        )
        return 0

    def greet_seq(r, _):
        pl.semaphore_signal(
            barrier, inc=1, device_id={"seq": lax.rem(seq + r, n_seq)}, device_id_type=MESH
        )
        return 0

    lax.fori_loop(1, n_seq, greet_seq, 0)
    lax.fori_loop(1, n_head, greet_head, 0)

    loads[0].wait()
    lane4 = lax.broadcasted_iota(jnp.int32, (HEADS, CHUNK), 1)
    pieces = []
    for i in range(chunks):
        piece = decay[:, i * CHUNK : (i + 1) * CHUNK]
        for half in range(2):
            begins = doc_ref[seq * (tokens // SPAN) + 2 * i + half] != 0
            drop = jnp.where(begins, RESET, 0.0)
            piece = piece - jnp.where(lane4 == half * SPAN, drop, 0.0)
        pieces.append(piece)
    run = jnp.concatenate(pieces, axis=0)
    lane = lax.broadcasted_iota(jnp.int32, run.shape, 1)
    shift = 1
    while shift < CHUNK:
        run = run + jnp.where(lane >= shift, pltpu.roll(run, shift, 1), 0.0)
        shift *= 2
    total = jnp.broadcast_to(run[:, CHUNK - 1 : CHUNK], run.shape)
    ds[...] = jnp.zeros_like(ds)
    before = jnp.zeros((HEADS, CHUNK), F32)
    after = jnp.zeros((HEADS, CHUNK), F32)
    for i in range(chunks):
        part = slice(i * HEADS, (i + 1) * HEADS)
        ds[i, 0:HEADS, :] = run[part]
        tot[i] = total[part]
        query_w[i] = jnp.exp(before + run[part])
        before = before + total[part]
    for i in reversed(range(chunks)):
        part = slice(i * HEADS, (i + 1) * HEADS)
        key_w[i] = jnp.exp(after + (total[part] - run[part]))
        after = after + total[part]
    own_decay[...] = jnp.zeros_like(own_decay)
    own_decay[0:HEADS, :] = before

    def scaled(i, weights):
        parts = [
            value_t[i, h * DIM : (h + 1) * DIM, :].astype(F32) * weights[h : h + 1, :]
            for h in range(HEADS)
        ]
        return jnp.concatenate(parts, axis=0).astype(BF16)

    def at(i):
        return pl.ds(pl.multiple_of(i * CHUNK, CHUNK), CHUNK)

    loads[2].wait()
    wide[...] = pair[0].reshape(2 * tokens, STATE).astype(F32)
    keys[...] = wide[pl.ds(lax.rem(group, 2), tokens, stride=2), :].astype(BF16)
    loads[1].wait()
    own_state[...] = jnp.zeros_like(own_state)

    def state_step(i, _):
        value_t[i] = raw[at(i), :].T
        own_state[...] += dot(scaled(i, key_w[i]), keys[at(i), :])
        return 0

    lax.fori_loop(0, chunks, state_step, 0)

    pl.semaphore_wait(barrier, n_seq - 1 + n_head - 1)

    swap = pltpu.make_async_remote_copy(
        src_ref=own_state, dst_ref=sib_state, send_sem=swap_sem.at[0], recv_sem=swap_sem.at[1],
        device_id={"seq": 2 * z + 1 - core}, device_id_type=MESH,
    )
    swap.start()

    def decay_copy(other, slot):
        return pltpu.make_async_remote_copy(
            src_ref=own_decay, dst_ref=all_decay.at[slot], send_sem=decay_send.at[other],
            recv_sem=decay_recv.at[slot], device_id={"seq": other}, device_id_type=MESH,
        )

    def send_decay(r, _):
        decay_copy(lax.rem(seq + r, n_seq), seq).start()
        return 0

    lax.fori_loop(1, n_seq, send_decay, 0)
    all_decay[pl.ds(seq, 1)] = own_decay[...][None]

    loads[3].wait()
    wide[...] = pair[1].reshape(2 * tokens, STATE).astype(F32)

    def turn_queries(i, _):
        start = lax.rem(group, 2) + i * (2 * CHUNK)
        query_t[i] = wide[pl.ds(start, CHUNK, stride=2), :].T.astype(BF16)
        return 0

    lax.fori_loop(0, chunks, turn_queries, 0)

    def wait_decay(r, _):
        other = lax.rem(seq + r, n_seq)
        decay_copy(other, other).wait_recv()
        return 0

    lax.fori_loop(1, n_seq, wait_decay, 0)
    swap.wait_recv()

    is_upper = core == 1
    half = width // 2
    mine = pl.ds(pl.multiple_of(core * half, half), half)
    theirs = pl.ds(pl.multiple_of((1 - core) * half, half), half)
    upper_decay = all_decay[2 * z + 1]
    through = jnp.exp(upper_decay)
    parts = []
    for j in range(2):
        rows = pl.ds(pl.multiple_of(core * half + j * DIM, DIM), DIM)
        fade = jnp.where(is_upper, through[2 + j : 3 + j, :], through[j : j + 1, :])
        here, there = own_state[rows, :], sib_state[rows, :]
        low = jnp.where(is_upper, there, here)
        high = jnp.where(is_upper, here, there)
        parts.append(low * fade + high)
    chip_state[...] = jnp.concatenate(parts, axis=0).astype(BF16)

    def chip_copy(other, slot):
        return pltpu.make_async_remote_copy(
            src_ref=chip_state, dst_ref=chip_states.at[slot], send_sem=chip_send.at[other],
            recv_sem=chip_recv.at[slot], device_id={"seq": 2 * other + core}, device_id_type=MESH,
        )

    def send_chip(r, _):
        chip_copy(lax.rem(z + r, n_z), z).start()
        return 0

    lax.fori_loop(1, n_z, send_chip, 0)

    gap = jnp.zeros((8, CHUNK), F32)
    for j in reversed(range(n_z)):
        coef[j] = jnp.where(j < z, jnp.exp(gap), 0.0)
        gap = gap + jnp.where(j < z, all_decay[2 * j] + all_decay[2 * j + 1], 0.0)
    levels[0] = jnp.where(is_upper, sib_state[...], 0.0).astype(BF16)

    loads[4].wait()
    loads[5].wait()
    acc[...] = jnp.zeros_like(acc)
    sub_i = lax.broadcasted_iota(jnp.int32, (CHUNK, CHUNK), 0)
    lane_i = lax.broadcasted_iota(jnp.int32, (CHUNK, CHUNK), 1)
    causal = sub_i <= lane_i
    early = sub_i < SPAN
    first_half = lax.broadcasted_iota(jnp.int32, (1, CHUNK), 1) < SPAN
    local_levels = acc.shape[0]

    def near_step(i, _):
        g = gate[at(i), :].astype(F32)
        silu[i] = g / (1.0 + jnp.exp(-g))
        turned = query_t[i]
        block = keys[at(i), :]
        scores = dot(block, turned)
        run_i = ds[i]
        columns = run_i.T
        weight = jnp.exp(run_i)
        tot_i = tot[i]
        into = dot(
            acc[...].reshape(local_levels * width, STATE).astype(BF16), turned
        ).reshape(local_levels, width, CHUNK)
        for h in range(HEADS):
            rows = slice(h * DIM, (h + 1) * DIM)
            fall = run_i[h : h + 1, :] - jnp.broadcast_to(columns[:, h : h + 1], (CHUNK, CHUNK))
            same = level[0, h : h + 1, at(i)]
            cross = jnp.where(first_half, same, level[1, h : h + 1, at(i)])
            mixed = jnp.exp(jnp.where(causal, fall, -1e30)) * jnp.where(early, cross, same) * scores
            result = dot(value_t[i, rows, :], mixed.astype(BF16))
            for k in range(local_levels):
                on = (lax.shift_right_logical(i, k) & 1).astype(F32)
                factor = level[2 + k, h : h + 1, at(i)] * weight[h : h + 1, :] * on
                result = result + into[k, rows, :] * factor
            near[i, rows, :] = result
        state = dot(scaled(i, jnp.exp(tot_i - run_i[0:HEADS])), block)
        keep = jnp.exp(tot_i)
        for k in range(local_levels):
            low = (1 - (lax.shift_right_logical(i, k) & 1)).astype(F32)
            held = (lax.rem(i, 2 ** (k + 1)) != 0).astype(F32)
            for h in range(HEADS):
                rows = slice(h * DIM, (h + 1) * DIM)
                acc[k, rows, :] = acc[k, rows, :] * (keep[h : h + 1, :] * held) + state[rows, :] * low
        return 0

    lax.fori_loop(0, chunks, near_step, 0)

    def wait_chip(r, _):
        other = lax.rem(z + r, n_z)
        chip_copy(other, other).wait_recv()
        return 0

    lax.fori_loop(1, n_z, wait_chip, 0)
    for k in range(far_levels - 1):
        first = (lax.shift_right_logical(z, k) ^ 1) * 2**k
        for j in range(2):
            total_j = jnp.zeros((DIM, STATE), F32)
            for n in range(2**k):
                row = coef[first + n]
                fade = jnp.where(is_upper, row[2 + j : 3 + j, :], row[j : j + 1, :])
                total_j = total_j + chip_states[first + n, j * DIM : (j + 1) * DIM, :].astype(F32) * fade
            own_levels[k, j * DIM : (j + 1) * DIM, :] = total_j.astype(BF16)
    share = pltpu.make_async_remote_copy(
        src_ref=own_levels, dst_ref=sib_levels, send_sem=swap_sem.at[2], recv_sem=swap_sem.at[3],
        device_id={"seq": 2 * z + 1 - core}, device_id_type=MESH,
    )
    share.start()
    for k in range(far_levels - 1):
        levels[1 + k, mine, :] = own_levels[k]
    share.wait_recv()
    for k in range(far_levels - 1):
        levels[1 + k, theirs, :] = sib_levels[k]

    def row_copy(target, source, i, k):
        return pltpu.make_async_remote_copy(
            src_ref=outgoing.at[i, pl.ds(pl.multiple_of(k * rows_out, rows_out), rows_out), :],
            dst_ref=arrived.at[:, pl.ds(pl.multiple_of(source * width, width), width)],
            send_sem=rows_send.at[target], recv_sem=rows_recv.at[source],
            device_id={"head": target}, device_id_type=MESH,
        )

    own_chunk = me // per_chunk
    base = level.shape[0] - far_levels

    def far_step(r, _):
        i = lax.rem(own_chunk + r, chunks)
        into = dot(
            levels[...].reshape(far_levels * width, STATE), query_t[i]
        ).reshape(far_levels, width, CHUNK)
        weight = query_w[i]
        further = weight * jnp.where(is_upper, jnp.exp(all_decay[2 * z])[0:HEADS], 1.0)
        columns = []
        for h in range(HEADS):
            rows = slice(h * DIM, (h + 1) * DIM)
            result = near[i, rows, :]
            for k in range(far_levels):
                from_start = weight if k == 0 else further
                factor = level[base + k, h : h + 1, at(i)] * from_start[h : h + 1, :]
                result = result + into[k, rows, :] * factor
            columns.append(result)
        mixed = jnp.concatenate(columns, axis=0).T
        outgoing[i] = (mixed * silu[i]).astype(BF16)
        for k in range(per_chunk):
            target = i * per_chunk + k

            @pl.when(target != me)
            def _():
                row_copy(target, me, i, k).start()

            @pl.when(target == me)
            def _():
                arrived[:, pl.ds(pl.multiple_of(me * width, width), width)] = outgoing[
                    i, k * rows_out : (k + 1) * rows_out, :
                ]

        return 0

    lax.fori_loop(0, chunks, far_step, 0)

    loads[6].wait()
    group_width = PER_GROUP * DIM
    per_group = group_width // width
    groups = n_head // per_group

    def norm_step(r, _):
        g = lax.rem(me // per_group - r + groups, groups)
        for k in range(per_group):
            source = g * per_group + k

            @pl.when(source != me)
            def _():
                row_copy(source, source, 0, 0).wait_recv()

        x = arrived[:, pl.ds(pl.multiple_of(g * group_width, group_width), group_width)].astype(F32)
        inverse = lax.rsqrt(jnp.sum(x * x, axis=1, keepdims=True) * (1.0 / group_width) + 1e-05)
        for k in range(group_width // CHUNK):
            y = x[:, k * CHUNK : (k + 1) * CHUNK] * inverse * gain[pl.ds(g * (group_width // CHUNK) + k, 1), :]
            out_ref[:, pl.ds(pl.multiple_of(g * group_width + k * CHUNK, CHUNK), CHUNK)] = y.astype(BF16)
        return 0

    lax.fori_loop(0, groups, norm_step, 0)

    def drain_rows(r, _):
        row_copy(lax.rem(me + r, n_head), me, 0, 0).wait_send()
        return 0

    lax.fori_loop(1, n_head, drain_rows, 0)

    def drain_decay(r, _):
        decay_copy(lax.rem(seq + r, n_seq), seq).wait_send()
        return 0

    lax.fori_loop(1, n_seq, drain_decay, 0)

    def drain_chip(r, _):
        chip_copy(lax.rem(z + r, n_z), z).wait_send()
        return 0

    lax.fori_loop(1, n_z, drain_chip, 0)
    swap.wait_send()
    share.wait_send()


def solution(mesh):
    n_seq, n_head = mesh.shape["seq"], mesh.shape["head"]
    n_z = n_seq // 2

    def body(values, gate_z, b_keys, c_queries, log_decay, level_weight, doc_start, norm_gain):
        tokens, width = values.shape
        chunks = tokens // CHUNK
        n_levels = level_weight.shape[2]
        far_levels = n_z.bit_length()
        local_levels = chunks.bit_length() - 1
        groups = b_keys.shape[1]
        any_space = pl.BlockSpec(memory_space=pl.ANY)
        rows = tokens // n_head
        dma = pltpu.SemaphoreType.DMA

        def run(*args):
            return kernel(n_seq, n_head, *args)

        return pl.pallas_call(
            run,
            out_shape=jax.ShapeDtypeStruct((rows, n_head * width), BF16),
            in_specs=[any_space] * 7 + [pl.BlockSpec(memory_space=pltpu.SMEM)],
            out_specs=pl.BlockSpec(memory_space=pltpu.VMEM),
            scratch_shapes=[
                pltpu.VMEM((2, tokens, 2, STATE), BF16),
                pltpu.VMEM((2 * tokens, STATE), F32),
                pltpu.VMEM((tokens, STATE), BF16),
                pltpu.VMEM((chunks, STATE, CHUNK), BF16),
                pltpu.VMEM((tokens, width), BF16),
                pltpu.VMEM((chunks, width, CHUNK), BF16),
                pltpu.VMEM((tokens, width), BF16),
                pltpu.VMEM((chunks, CHUNK, width), F32),
                pltpu.VMEM((HEADS, tokens), F32),
                pltpu.VMEM((n_levels, HEADS, tokens), F32),
                pltpu.VMEM((n_head * width // CHUNK, CHUNK), F32),
                pltpu.VMEM((chunks, 8, CHUNK), F32),
                pltpu.VMEM((chunks, HEADS, CHUNK), F32),
                pltpu.VMEM((chunks, HEADS, CHUNK), F32),
                pltpu.VMEM((chunks, HEADS, CHUNK), F32),
                pltpu.VMEM((chunks, width, CHUNK), F32),
                pltpu.VMEM((local_levels, width, STATE), F32),
                pltpu.VMEM((width, STATE), F32),
                pltpu.VMEM((width, STATE), F32),
                pltpu.VMEM((8, CHUNK), F32),
                pltpu.VMEM((n_seq, 8, CHUNK), F32),
                pltpu.VMEM((width // 2, STATE), BF16),
                pltpu.VMEM((n_z, width // 2, STATE), BF16),
                pltpu.VMEM((n_z, 8, CHUNK), F32),
                pltpu.VMEM((far_levels - 1, width // 2, STATE), BF16),
                pltpu.VMEM((far_levels - 1, width // 2, STATE), BF16),
                pltpu.VMEM((far_levels, width, STATE), BF16),
                pltpu.VMEM((chunks, CHUNK, width), BF16),
                pltpu.VMEM((rows, n_head * width), BF16),
                dma((7,)),
                dma((4,)),
                dma((n_seq,)),
                dma((n_seq,)),
                dma((n_z,)),
                dma((n_z,)),
                dma((n_head,)),
                dma((n_head,)),
            ],
            compiler_params=pltpu.CompilerParams(collective_id=0, has_side_effects=True),
        )(
            b_keys.reshape(tokens, groups // 2, 2, STATE),
            c_queries.reshape(tokens, groups // 2, 2, STATE),
            values,
            gate_z,
            log_decay.T,
            level_weight.transpose(2, 1, 0),
            norm_gain.reshape(n_head * width // CHUNK, CHUNK),
            doc_start,
        )

    in_specs = (
        P("seq", "head"),
        P("seq", "head"),
        P("seq", None, None),
        P("seq", None, None),
        P("seq", "head"),
        P("seq", "head", None),
        P(),
        P(),
    )
    out_specs = P(("seq", "head"), None)
    return jax.shard_map(body, mesh=mesh, in_specs=in_specs, out_specs=out_specs, check_vma=False)
```

profile of v0, /device:TPU:1, one launch (start us, length us, event | category | flops | bytes accessed | tf_op | source)
XLA Modules:
  0.0 48.5 jit_solution(9311399709001379305)
XLA Ops:
  0.0 46.6 %shard_map.82 = bf16[32,8192]{1,0:T(8,128)(2,1)} custom-call(bf16[1024,4,2,128]{3,2,1,0:T(2,128)(2,1)} %bitcast.5, bf16[1024,4,2,128]{3,2,1,0:T(2,128)(2,1)} %bitcast.6, bf16[1024,256]{1,0:T(8,128)(2,1)} %args_2_.4, bf16[1024,256]{1,0:T(8,128)(2,1)} %args_3_.4, f32[4,1024]{1,0:T(4,128)} %bitcast.9, f32[9,4,1024]{2,1,0:T(4,128)} %bitcast.7, ...), custom_call_target="tpu_custom_call" | custom-call | tf_op jit(solution)/shard_map/pallas_call | solution.py:382
  46.6 1.9 %copy.10 = bf16[32,8192]{1,0:T(8,128)(2,1)} copy(bf16[32,8192]{1,0:T(8,128)(2,1)} %shard_map.82) | data formatting | bytes 1048576
where the time goes:
time: 48.7 us; the launch traced here: 48.5 us
  Pallas kernels  46.6 us (96%)
  local copies, waits for them, and re-layouts  1.87 us (4%)
    pallas_call x1, Pallas kernels, body(): pl.pallas_call(run, out_shape=jax.ShapeDtypeStruct((rows, n_head * width)...  46.6 us
    unnamed x1, local copies, waits for them, and re-layouts  1.87 us

commit v1 on v0

--- a/solution.py
+++ b/solution.py
@@ -14,6 +14,7 @@
 DIM = 64
 STATE = 128
 PER_GROUP = 16
+PAIRS = HEADS // 2
 RESET = 128.0
 
 
@@ -38,7 +39,6 @@
     chunks = tokens // CHUNK
     width = HEADS * DIM
     rows_out = tokens // n_head
-    per_chunk = CHUNK // rows_out
 
     loads = [
         pltpu.make_async_copy(decay_hbm, decay, load_sem.at[0]),
@@ -165,38 +165,40 @@
     swap.wait_recv()
 
     is_upper = core == 1
-    half = width // 2
-    mine = pl.ds(pl.multiple_of(core * half, half), half)
-    theirs = pl.ds(pl.multiple_of((1 - core) * half, half), half)
     upper_decay = all_decay[2 * z + 1]
     through = jnp.exp(upper_decay)
-    parts = []
-    for j in range(2):
-        rows = pl.ds(pl.multiple_of(core * half + j * DIM, DIM), DIM)
-        fade = jnp.where(is_upper, through[2 + j : 3 + j, :], through[j : j + 1, :])
+    mine = pl.ds(pl.multiple_of(core * DIM, DIM), DIM)
+    theirs = pl.ds(pl.multiple_of((1 - core) * DIM, DIM), DIM)
+    for p in range(PAIRS):
+        rows = pl.ds(pl.multiple_of(p * 2 * DIM + core * DIM, DIM), DIM)
+        fade = jnp.where(is_upper, through[2 * p + 1 : 2 * p + 2, :], through[2 * p : 2 * p + 1, :])
         here, there = own_state[rows, :], sib_state[rows, :]
         low = jnp.where(is_upper, there, here)
         high = jnp.where(is_upper, here, there)
-        parts.append(low * fade + high)
-    chip_state[...] = jnp.concatenate(parts, axis=0).astype(BF16)
-
-    def chip_copy(other, slot):
+        chip_state[p] = (low * fade + high).astype(BF16)
+
+    def chip_copy(p, other, slot):
         return pltpu.make_async_remote_copy(
-            src_ref=chip_state, dst_ref=chip_states.at[slot], send_sem=chip_send.at[other],
-            recv_sem=chip_recv.at[slot], device_id={"seq": 2 * other + core}, device_id_type=MESH,
-        )
-
-    def send_chip(r, _):
-        chip_copy(lax.rem(z + r, n_z), z).start()
-        return 0
-
-    lax.fori_loop(1, n_z, send_chip, 0)
+            src_ref=chip_state.at[p], dst_ref=chip_states.at[p, slot],
+            send_sem=chip_send.at[p, other], recv_sem=chip_recv.at[p, slot],
+            device_id={"seq": 2 * other + core}, device_id_type=MESH,
+        )
+
+    for p in range(PAIRS):
+
+        def send_chip(r, _):
+            chip_copy(p, lax.rem(z + r, n_z), z).start()
+            return 0
+
+        lax.fori_loop(1, n_z, send_chip, 0)
 
     gap = jnp.zeros((8, CHUNK), F32)
     for j in reversed(range(n_z)):
         coef[j] = jnp.where(j < z, jnp.exp(gap), 0.0)
         gap = gap + jnp.where(j < z, all_decay[2 * j] + all_decay[2 * j + 1], 0.0)
-    levels[0] = jnp.where(is_upper, sib_state[...], 0.0).astype(BF16)
+    for p in range(PAIRS):
+        rows = slice(p * 2 * DIM, (p + 1) * 2 * DIM)
+        levels[p, 0] = jnp.where(is_upper, sib_state[rows, :], 0.0).astype(BF16)
 
     loads[4].wait()
     loads[5].wait()
@@ -210,7 +212,7 @@
 
     def near_step(i, _):
         g = gate[at(i), :].astype(F32)
-        silu[i] = g / (1.0 + jnp.exp(-g))
+        silu[at(i), :] = g / (1.0 + jnp.exp(-g))
         turned = query_t[i]
         block = keys[at(i), :]
         scores = dot(block, turned)
@@ -245,77 +247,89 @@
 
     lax.fori_loop(0, chunks, near_step, 0)
 
-    def wait_chip(r, _):
-        other = lax.rem(z + r, n_z)
-        chip_copy(other, other).wait_recv()
-        return 0
-
-    lax.fori_loop(1, n_z, wait_chip, 0)
-    for k in range(far_levels - 1):
-        first = (lax.shift_right_logical(z, k) ^ 1) * 2**k
-        for j in range(2):
-            total_j = jnp.zeros((DIM, STATE), F32)
+    def row_copy(p, target, source):
+        return pltpu.make_async_remote_copy(
+            src_ref=outgoing.at[p, pl.ds(pl.multiple_of(target * rows_out, rows_out), rows_out), :],
+            dst_ref=arrived.at[:, pl.ds(pl.multiple_of(source * width + p * CHUNK, CHUNK), CHUNK)],
+            send_sem=rows_send.at[p, target], recv_sem=rows_recv.at[p, source],
+            device_id={"head": target}, device_id_type=MESH,
+        )
+
+    wide_chunk = 2 * CHUNK
+    per_chunk = wide_chunk // rows_out
+    own_chunk = me // per_chunk
+    base = level.shape[0] - far_levels
+    shares = []
+    beyond = jnp.where(is_upper, jnp.exp(all_decay[2 * z])[0:HEADS], 1.0)
+
+    for p in range(PAIRS):
+        def wait_chip(r, _):
+            other = lax.rem(z + r, n_z)
+            chip_copy(p, other, other).wait_recv()
+            return 0
+
+        lax.fori_loop(1, n_z, wait_chip, 0)
+        for k in range(far_levels - 1):
+            first = (lax.shift_right_logical(z, k) ^ 1) * 2**k
+            sums = jnp.zeros((DIM, STATE), F32)
             for n in range(2**k):
                 row = coef[first + n]
-                fade = jnp.where(is_upper, row[2 + j : 3 + j, :], row[j : j + 1, :])
-                total_j = total_j + chip_states[first + n, j * DIM : (j + 1) * DIM, :].astype(F32) * fade
-            own_levels[k, j * DIM : (j + 1) * DIM, :] = total_j.astype(BF16)
-    share = pltpu.make_async_remote_copy(
-        src_ref=own_levels, dst_ref=sib_levels, send_sem=swap_sem.at[2], recv_sem=swap_sem.at[3],
-        device_id={"seq": 2 * z + 1 - core}, device_id_type=MESH,
-    )
-    share.start()
-    for k in range(far_levels - 1):
-        levels[1 + k, mine, :] = own_levels[k]
-    share.wait_recv()
-    for k in range(far_levels - 1):
-        levels[1 + k, theirs, :] = sib_levels[k]
-
-    def row_copy(target, source, i, k):
-        return pltpu.make_async_remote_copy(
-            src_ref=outgoing.at[i, pl.ds(pl.multiple_of(k * rows_out, rows_out), rows_out), :],
-            dst_ref=arrived.at[:, pl.ds(pl.multiple_of(source * width, width), width)],
-            send_sem=rows_send.at[target], recv_sem=rows_recv.at[source],
-            device_id={"head": target}, device_id_type=MESH,
-        )
-
-    own_chunk = me // per_chunk
-    base = level.shape[0] - far_levels
-
-    def far_step(r, _):
-        i = lax.rem(own_chunk + r, chunks)
-        into = dot(
-            levels[...].reshape(far_levels * width, STATE), query_t[i]
-        ).reshape(far_levels, width, CHUNK)
-        weight = query_w[i]
-        further = weight * jnp.where(is_upper, jnp.exp(all_decay[2 * z])[0:HEADS], 1.0)
-        columns = []
-        for h in range(HEADS):
-            rows = slice(h * DIM, (h + 1) * DIM)
-            result = near[i, rows, :]
-            for k in range(far_levels):
-                from_start = weight if k == 0 else further
-                factor = level[base + k, h : h + 1, at(i)] * from_start[h : h + 1, :]
-                result = result + into[k, rows, :] * factor
-            columns.append(result)
-        mixed = jnp.concatenate(columns, axis=0).T
-        outgoing[i] = (mixed * silu[i]).astype(BF16)
-        for k in range(per_chunk):
-            target = i * per_chunk + k
-
-            @pl.when(target != me)
-            def _():
-                row_copy(target, me, i, k).start()
-
-            @pl.when(target == me)
-            def _():
-                arrived[:, pl.ds(pl.multiple_of(me * width, width), width)] = outgoing[
-                    i, k * rows_out : (k + 1) * rows_out, :
-                ]
-
-        return 0
-
-    lax.fori_loop(0, chunks, far_step, 0)
+                fade = jnp.where(is_upper, row[2 * p + 1 : 2 * p + 2, :], row[2 * p : 2 * p + 1, :])
+                sums = sums + chip_states[p, first + n].astype(F32) * fade
+            own_levels[p, k] = sums.astype(BF16)
+        share = pltpu.make_async_remote_copy(
+            src_ref=own_levels.at[p], dst_ref=sib_levels.at[p], send_sem=swap_sem.at[2 + 2 * p],
+            recv_sem=swap_sem.at[3 + 2 * p], device_id={"seq": 2 * z + 1 - core},
+            device_id_type=MESH,
+        )
+        share.start()
+        shares.append(share)
+        for k in range(far_levels - 1):
+            levels[p, 1 + k, mine, :] = own_levels[p, k]
+        share.wait_recv()
+        for k in range(far_levels - 1):
+            levels[p, 1 + k, theirs, :] = sib_levels[p, k]
+
+        def far_step(r, _):
+            i = lax.rem(own_chunk + r, chunks // 2)
+            tokens_i = pl.ds(pl.multiple_of(i * wide_chunk, wide_chunk), wide_chunk)
+            queries = jnp.concatenate([query_t[2 * i], query_t[2 * i + 1]], axis=1)
+            into = dot(
+                levels[p].reshape(far_levels * 2 * DIM, STATE), queries
+            ).reshape(far_levels, 2 * DIM, wide_chunk)
+            weights = [query_w[2 * i], query_w[2 * i + 1]]
+            weight = jnp.concatenate(weights, axis=1)
+            further = jnp.concatenate([w * beyond for w in weights], axis=1)
+            columns = []
+            for j in range(2):
+                h = 2 * p + j
+                rows = slice(h * DIM, (h + 1) * DIM)
+                result = jnp.concatenate([near[2 * i, rows, :], near[2 * i + 1, rows, :]], axis=1)
+                for k in range(far_levels):
+                    from_start = weight if k == 0 else further
+                    factor = level[base + k, h : h + 1, tokens_i] * from_start[h : h + 1, :]
+                    result = result + into[k, j * DIM : (j + 1) * DIM, :] * factor
+                columns.append(result)
+            mixed = jnp.concatenate(columns, axis=0).T
+            gates = silu[tokens_i, p * CHUNK : (p + 1) * CHUNK]
+            outgoing[p, tokens_i, :] = (mixed * gates).astype(BF16)
+
+            def send_rows(k, _):
+                target = i * per_chunk + lax.rem(me + k, per_chunk)
+
+                @pl.when(target != me)
+                def _():
+                    row_copy(p, target, me).start()
+
+                return 0
+
+            lax.fori_loop(0, per_chunk, send_rows, 0)
+            return 0
+
+        lax.fori_loop(0, chunks // 2, far_step, 0)
+        arrived[:, pl.ds(pl.multiple_of(me * width + p * CHUNK, CHUNK), CHUNK)] = outgoing[
+            p, pl.ds(pl.multiple_of(me * rows_out, rows_out), rows_out), :
+        ]
 
     loads[6].wait()
     group_width = PER_GROUP * DIM
@@ -329,7 +343,8 @@
 
             @pl.when(source != me)
             def _():
-                row_copy(source, source, 0, 0).wait_recv()
+                for p in range(PAIRS):
+                    row_copy(p, source, source).wait_recv()
 
         x = arrived[:, pl.ds(pl.multiple_of(g * group_width, group_width), group_width)].astype(F32)
         inverse = lax.rsqrt(jnp.sum(x * x, axis=1, keepdims=True) * (1.0 / group_width) + 1e-05)
@@ -341,7 +356,8 @@
     lax.fori_loop(0, groups, norm_step, 0)
 
     def drain_rows(r, _):
-        row_copy(lax.rem(me + r, n_head), me, 0, 0).wait_send()
+        for p in range(PAIRS):
+            row_copy(p, lax.rem(me + r, n_head), me).wait_send()
         return 0
 
     lax.fori_loop(1, n_head, drain_rows, 0)
@@ -353,12 +369,14 @@
     lax.fori_loop(1, n_seq, drain_decay, 0)
 
     def drain_chip(r, _):
-        chip_copy(lax.rem(z + r, n_z), z).wait_send()
+        for p in range(PAIRS):
+            chip_copy(p, lax.rem(z + r, n_z), z).wait_send()
         return 0
 
     lax.fori_loop(1, n_z, drain_chip, 0)
     swap.wait_send()
-    share.wait_send()
+    for share in shares:
+        share.wait_send()
 
 
 def solution(mesh):
@@ -392,7 +410,7 @@
                 pltpu.VMEM((tokens, width), BF16),
                 pltpu.VMEM((chunks, width, CHUNK), BF16),
                 pltpu.VMEM((tokens, width), BF16),
-                pltpu.VMEM((chunks, CHUNK, width), F32),
+                pltpu.VMEM((tokens, width), F32),
                 pltpu.VMEM((HEADS, tokens), F32),
                 pltpu.VMEM((n_levels, HEADS, tokens), F32),
                 pltpu.VMEM((n_head * width // CHUNK, CHUNK), F32),
@@ -406,22 +424,22 @@
                 pltpu.VMEM((width, STATE), F32),
                 pltpu.VMEM((8, CHUNK), F32),
                 pltpu.VMEM((n_seq, 8, CHUNK), F32),
-                pltpu.VMEM((width // 2, STATE), BF16),
-                pltpu.VMEM((n_z, width // 2, STATE), BF16),
+                pltpu.VMEM((PAIRS, DIM, STATE), BF16),
+                pltpu.VMEM((PAIRS, n_z, DIM, STATE), BF16),
                 pltpu.VMEM((n_z, 8, CHUNK), F32),
-                pltpu.VMEM((far_levels - 1, width // 2, STATE), BF16),
-                pltpu.VMEM((far_levels - 1, width // 2, STATE), BF16),
-                pltpu.VMEM((far_levels, width, STATE), BF16),
-                pltpu.VMEM((chunks, CHUNK, width), BF16),
+                pltpu.VMEM((PAIRS, far_levels - 1, DIM, STATE), BF16),
+                pltpu.VMEM((PAIRS, far_levels - 1, DIM, STATE), BF16),
+                pltpu.VMEM((PAIRS, far_levels, 2 * DIM, STATE), BF16),
+                pltpu.VMEM((PAIRS, tokens, CHUNK), BF16),
                 pltpu.VMEM((rows, n_head * width), BF16),
                 dma((7,)),
-                dma((4,)),
+                dma((2 + 2 * PAIRS,)),
                 dma((n_seq,)),
                 dma((n_seq,)),
-                dma((n_z,)),
-                dma((n_z,)),
-                dma((n_head,)),
-                dma((n_head,)),
+                dma((PAIRS, n_z)),
+                dma((PAIRS, n_z)),
+                dma((PAIRS, n_head)),
+                dma((PAIRS, n_head)),
             ],
             compiler_params=pltpu.CompilerParams(collective_id=0, has_side_effects=True),
         )(

time: 48.7 us -> 50.9 us (1.045)
  Pallas kernels: 46.6 us -> 48.9 us
    pallas_call x1, Pallas kernels: 46.6 us -> 48.9 us  [body(): pl.pallas_call(run, out_shape=jax.ShapeDtypeStruct((rows, n_head * width)...]
where the time goes in v1:
time: 50.9 us; the launch traced here: 50.7 us
  Pallas kernels  48.9 us (96%)
  local copies, waits for them, and re-layouts  1.87 us (4%)
    pallas_call x1, Pallas kernels, body(): pl.pallas_call(run, out_shape=jax.ShapeDtypeStruct((rows, n_head * width)...  48.9 us
    unnamed x1, local copies, waits for them, and re-layouts  1.87 us

profile of v1, /device:TPU:1, one launch (start us, length us, event | category | flops | bytes accessed | tf_op | source)
XLA Modules:
  0.0 50.7 jit_solution(11432958082515614043)
XLA Ops:
  0.0 48.9 %shard_map.82 = bf16[32,8192]{1,0:T(8,128)(2,1)} custom-call(bf16[1024,4,2,128]{3,2,1,0:T(2,128)(2,1)} %bitcast.5, bf16[1024,4,2,128]{3,2,1,0:T(2,128)(2,1)} %bitcast.6, bf16[1024,256]{1,0:T(8,128)(2,1)} %args_2_.4, bf16[1024,256]{1,0:T(8,128)(2,1)} %args_3_.4, f32[4,1024]{1,0:T(4,128)} %bitcast.9, f32[9,4,1024]{2,1,0:T(4,128)} %bitcast.7, ...), custom_call_target="tpu_custom_call" | custom-call | tf_op jit(solution)/shard_map/pallas_call | solution.py:400
  48.9 1.9 %copy.10 = bf16[32,8192]{1,0:T(8,128)(2,1)} copy(bf16[32,8192]{1,0:T(8,128)(2,1)} %shard_map.82) | data formatting | bytes 1048576

commit v2 on v1

--- a/solution.py
+++ b/solution.py
@@ -156,12 +156,8 @@
 
     lax.fori_loop(0, chunks, turn_queries, 0)
 
-    def wait_decay(r, _):
-        other = lax.rem(seq + r, n_seq)
-        decay_copy(other, other).wait_recv()
-        return 0
-
-    lax.fori_loop(1, n_seq, wait_decay, 0)
+    sibling = 2 * z + 1 - core
+    decay_copy(sibling, sibling).wait_recv()
     swap.wait_recv()
 
     is_upper = core == 1
@@ -184,18 +180,14 @@
             device_id={"seq": 2 * other + core}, device_id_type=MESH,
         )
 
-    for p in range(PAIRS):
-
+    def send_chips(p):
         def send_chip(r, _):
             chip_copy(p, lax.rem(z + r, n_z), z).start()
             return 0
 
         lax.fori_loop(1, n_z, send_chip, 0)
 
-    gap = jnp.zeros((8, CHUNK), F32)
-    for j in reversed(range(n_z)):
-        coef[j] = jnp.where(j < z, jnp.exp(gap), 0.0)
-        gap = gap + jnp.where(j < z, all_decay[2 * j] + all_decay[2 * j + 1], 0.0)
+    send_chips(0)
     for p in range(PAIRS):
         rows = slice(p * 2 * DIM, (p + 1) * 2 * DIM)
         levels[p, 0] = jnp.where(is_upper, sib_state[rows, :], 0.0).astype(BF16)
@@ -246,6 +238,23 @@
         return 0
 
     lax.fori_loop(0, chunks, near_step, 0)
+    for p in range(1, PAIRS):
+        send_chips(p)
+
+    def wait_decay(r, _):
+        other = lax.rem(seq + r, n_seq)
+
+        @pl.when(other != sibling)
+        def _():
+            decay_copy(other, other).wait_recv()
+
+        return 0
+
+    lax.fori_loop(1, n_seq, wait_decay, 0)
+    gap = jnp.zeros((8, CHUNK), F32)
+    for j in reversed(range(n_z)):
+        coef[j] = jnp.where(j < z, jnp.exp(gap), 0.0)
+        gap = gap + jnp.where(j < z, all_decay[2 * j] + all_decay[2 * j + 1], 0.0)
 
     def row_copy(p, target, source):
         return pltpu.make_async_remote_copy(

time: 50.9 us -> 45.9 us (0.902)
  Pallas kernels: 48.9 us -> 43.8 us
    pallas_call x1, Pallas kernels: 48.9 us -> 43.8 us  [body(): pl.pallas_call(run, out_shape=jax.ShapeDtypeStruct((rows, n_head * width)...]
where the time goes in v2:
time: 45.9 us; the launch traced here: 45.7 us
  Pallas kernels  43.8 us (95%)
  local copies, waits for them, and re-layouts  1.87 us (4%)
    pallas_call x1, Pallas kernels, body(): pl.pallas_call(run, out_shape=jax.ShapeDtypeStruct((rows, n_head * width)...  43.8 us
    unnamed x1, local copies, waits for them, and re-layouts  1.87 us

profile of v2, /device:TPU:1, one launch (start us, length us, event | category | flops | bytes accessed | tf_op | source)
XLA Modules:
  0.0 45.7 jit_solution(8919655633615863737)
XLA Ops:
  0.0 43.8 %shard_map.82 = bf16[32,8192]{1,0:T(8,128)(2,1)} custom-call(bf16[1024,4,2,128]{3,2,1,0:T(2,128)(2,1)} %bitcast.5, bf16[1024,4,2,128]{3,2,1,0:T(2,128)(2,1)} %bitcast.6, bf16[1024,256]{1,0:T(8,128)(2,1)} %args_2_.4, bf16[1024,256]{1,0:T(8,128)(2,1)} %args_3_.4, f32[4,1024]{1,0:T(4,128)} %bitcast.9, f32[9,4,1024]{2,1,0:T(4,128)} %bitcast.7, ...), custom_call_target="tpu_custom_call" | custom-call | tf_op jit(solution)/shard_map/pallas_call | solution.py:409
  43.8 1.9 %copy.10 = bf16[32,8192]{1,0:T(8,128)(2,1)} copy(bf16[32,8192]{1,0:T(8,128)(2,1)} %shard_map.82) | data formatting | bytes 1048576

commit v3 on v2

--- a/solution.py
+++ b/solution.py
@@ -15,6 +15,7 @@
 STATE = 128
 PER_GROUP = 16
 PAIRS = HEADS // 2
+SECTIONS = 4
 RESET = 128.0
 
 
@@ -23,8 +24,8 @@
 
 
 def kernel(
-    n_seq, n_head, b_hbm, c_hbm, v_hbm, g_hbm, decay_hbm, level_hbm, gain_hbm, doc_ref, out_ref,
-    pair, wide, keys, query_t, raw, value_t, gate, silu, decay, level, gain,
+    n_seq, n_head, b_hbm, c_hbm, v_hbm, g_hbm, decay_hbm, level_hbm, doc_ref, out_ref,
+    pair, wide, keys, query_t, raw, value_t, gate, silu, decay, level,
     ds, tot, key_w, query_w, near, acc, own_state, sib_state, own_decay, all_decay,
     chip_state, chip_states, coef, own_levels, sib_levels, levels, outgoing, arrived,
     load_sem, swap_sem, decay_send, decay_recv, chip_send, chip_recv, rows_send, rows_recv,
@@ -43,13 +44,19 @@
     loads = [
         pltpu.make_async_copy(decay_hbm, decay, load_sem.at[0]),
         pltpu.make_async_copy(v_hbm, raw, load_sem.at[1]),
-        pltpu.make_async_copy(b_hbm.at[:, group // 2], pair.at[0], load_sem.at[2]),
-        pltpu.make_async_copy(c_hbm.at[:, group // 2], pair.at[1], load_sem.at[3]),
-        pltpu.make_async_copy(level_hbm, level, load_sem.at[4]),
-        pltpu.make_async_copy(g_hbm, gate, load_sem.at[5]),
-        pltpu.make_async_copy(gain_hbm, gain, load_sem.at[6]),
+        pltpu.make_async_copy(c_hbm.at[:, group // 2], pair.at[1], load_sem.at[2]),
+        pltpu.make_async_copy(level_hbm, level, load_sem.at[3]),
+        pltpu.make_async_copy(g_hbm, gate, load_sem.at[4]),
     ]
-    for load in loads:
+    section = tokens // SECTIONS
+    key_loads = [
+        pltpu.make_async_copy(
+            b_hbm.at[pl.ds(j * section, section), group // 2],
+            pair.at[0, pl.ds(j * section, section)], load_sem.at[5 + j],
+        )
+        for j in range(SECTIONS)
+    ]
+    for load in loads[:2] + key_loads + loads[2:]:
         load.start()
 
     barrier = pltpu.get_barrier_semaphore()
@@ -112,9 +119,6 @@
     def at(i):
         return pl.ds(pl.multiple_of(i * CHUNK, CHUNK), CHUNK)
 
-    loads[2].wait()
-    wide[...] = pair[0].reshape(2 * tokens, STATE).astype(F32)
-    keys[...] = wide[pl.ds(lax.rem(group, 2), tokens, stride=2), :].astype(BF16)
     loads[1].wait()
     own_state[...] = jnp.zeros_like(own_state)
 
@@ -123,7 +127,14 @@
         own_state[...] += dot(scaled(i, key_w[i]), keys[at(i), :])
         return 0
 
-    lax.fori_loop(0, chunks, state_step, 0)
+    for j in range(SECTIONS):
+        rows = slice(j * section, (j + 1) * section)
+        key_loads[j].wait()
+        both = pair[0, rows].reshape(2 * section, STATE)
+        wide[2 * j * section : 2 * (j + 1) * section, :] = both.astype(F32)
+        start = lax.rem(group, 2) + 2 * j * section
+        keys[rows, :] = wide[pl.ds(start, section, stride=2), :].astype(BF16)
+        lax.fori_loop(j * chunks // SECTIONS, (j + 1) * chunks // SECTIONS, state_step, 0)
 
     pl.semaphore_wait(barrier, n_seq - 1 + n_head - 1)
 
@@ -146,7 +157,7 @@
     lax.fori_loop(1, n_seq, send_decay, 0)
     all_decay[pl.ds(seq, 1)] = own_decay[...][None]
 
-    loads[3].wait()
+    loads[2].wait()
     wide[...] = pair[1].reshape(2 * tokens, STATE).astype(F32)
 
     def turn_queries(i, _):
@@ -192,8 +203,8 @@
         rows = slice(p * 2 * DIM, (p + 1) * 2 * DIM)
         levels[p, 0] = jnp.where(is_upper, sib_state[rows, :], 0.0).astype(BF16)
 
+    loads[3].wait()
     loads[4].wait()
-    loads[5].wait()
     acc[...] = jnp.zeros_like(acc)
     sub_i = lax.broadcasted_iota(jnp.int32, (CHUNK, CHUNK), 0)
     lane_i = lax.broadcasted_iota(jnp.int32, (CHUNK, CHUNK), 1)
@@ -340,7 +351,6 @@
             p, pl.ds(pl.multiple_of(me * rows_out, rows_out), rows_out), :
         ]
 
-    loads[6].wait()
     group_width = PER_GROUP * DIM
     per_group = group_width // width
     groups = n_head // per_group
@@ -358,8 +368,8 @@
         x = arrived[:, pl.ds(pl.multiple_of(g * group_width, group_width), group_width)].astype(F32)
         inverse = lax.rsqrt(jnp.sum(x * x, axis=1, keepdims=True) * (1.0 / group_width) + 1e-05)
         for k in range(group_width // CHUNK):
-            y = x[:, k * CHUNK : (k + 1) * CHUNK] * inverse * gain[pl.ds(g * (group_width // CHUNK) + k, 1), :]
-            out_ref[:, pl.ds(pl.multiple_of(g * group_width + k * CHUNK, CHUNK), CHUNK)] = y.astype(BF16)
+            y = x[:, k * CHUNK : (k + 1) * CHUNK] * inverse
+            out_ref[:, pl.ds(pl.multiple_of(g * group_width + k * CHUNK, CHUNK), CHUNK)] = y
         return 0
 
     lax.fori_loop(0, groups, norm_step, 0)
@@ -406,10 +416,10 @@
         def run(*args):
             return kernel(n_seq, n_head, *args)
 
-        return pl.pallas_call(
+        whole = pl.pallas_call(
             run,
-            out_shape=jax.ShapeDtypeStruct((rows, n_head * width), BF16),
-            in_specs=[any_space] * 7 + [pl.BlockSpec(memory_space=pltpu.SMEM)],
+            out_shape=jax.ShapeDtypeStruct((rows, n_head * width), F32),
+            in_specs=[any_space] * 6 + [pl.BlockSpec(memory_space=pltpu.SMEM)],
             out_specs=pl.BlockSpec(memory_space=pltpu.VMEM),
             scratch_shapes=[
                 pltpu.VMEM((2, tokens, 2, STATE), BF16),
@@ -422,7 +432,6 @@
                 pltpu.VMEM((tokens, width), F32),
                 pltpu.VMEM((HEADS, tokens), F32),
                 pltpu.VMEM((n_levels, HEADS, tokens), F32),
-                pltpu.VMEM((n_head * width // CHUNK, CHUNK), F32),
                 pltpu.VMEM((chunks, 8, CHUNK), F32),
                 pltpu.VMEM((chunks, HEADS, CHUNK), F32),
                 pltpu.VMEM((chunks, HEADS, CHUNK), F32),
@@ -441,7 +450,7 @@
                 pltpu.VMEM((PAIRS, far_levels, 2 * DIM, STATE), BF16),
                 pltpu.VMEM((PAIRS, tokens, CHUNK), BF16),
                 pltpu.VMEM((rows, n_head * width), BF16),
-                dma((7,)),
+                dma((5 + SECTIONS,)),
                 dma((2 + 2 * PAIRS,)),
                 dma((n_seq,)),
                 dma((n_seq,)),
@@ -458,9 +467,9 @@
             gate_z,
             log_decay.T,
             level_weight.transpose(2, 1, 0),
-            norm_gain.reshape(n_head * width // CHUNK, CHUNK),
             doc_start,
         )
+        return (whole * norm_gain[None, :]).astype(BF16)
 
     in_specs = (
         P("seq", "head"),

time: 45.9 us -> 46.5 us (1.013)
  other arithmetic: 0 us -> 2.08 us
  local copies, waits for them, and re-layouts: 1.87 us -> 0.01 us
    convert_element_type x0 -> x1, other arithmetic: none -> 2.08 us  [body(): return (whole * norm_gain[None, :]).astype(BF16)]
    unnamed x1 -> x2, local copies, waits for them, and re-layouts: 1.87 us -> 0.01 us
where the time goes in v3:
time: 46.5 us; the launch traced here: 46.2 us
  Pallas kernels  44.1 us (95%)
  other arithmetic  2.08 us (4%)
    pallas_call x1, Pallas kernels, body(): pl.pallas_call(run, out_shape=jax.ShapeDtypeStruct((rows, n_head * width)...  44.1 us
    convert_element_type x1, other arithmetic, body(): return (whole * norm_gain[None, :]).astype(BF16)  2.08 us

profile of v3, /device:TPU:1, one launch (start us, length us, event | category | flops | bytes accessed | tf_op | source)
XLA Modules:
  0.0 46.2 jit_solution(3968609068997879649)
XLA Ops:
  0.0 0.0 copy-start
  0.0 44.1 %shard_map.82 = f32[32,8192]{1,0:T(8,128)} custom-call(bf16[1024,4,2,128]{3,2,1,0:T(2,128)(2,1)} %bitcast.4, bf16[1024,4,2,128]{3,2,1,0:T(2,128)(2,1)} %bitcast.5, bf16[1024,256]{1,0:T(8,128)(2,1)} %args_2_.4, bf16[1024,256]{1,0:T(8,128)(2,1)} %args_3_.4, f32[4,1024]{1,0:T(4,128)} %bitcast.7, f32[9,4,1024]{2,1,0:T(4,128)} %bitcast.6, s32[256]{0:T(256)} %args_6_.4), custom_call_target="tpu_custom_call" | custom-call | tf_op jit(solution)/shard_map/pallas_call | solution.py:419
  44.2 0.0 copy-done
  44.2 2.1 %multiply_convert_fusion = bf16[32,8192]{1,0:T(8,128)(2,1)} fusion(f32[32,8192]{1,0:T(8,128)} %shard_map.82, f32[8192]{0:T(1024)S(1)} %copy-done), kind=kLoop, calls=%fused_computation | loop fusion | flops 524288 | bytes 1605632 | tf_op jit(solution)/shard_map/convert_element_type | solution.py:472
Async XLA Ops:
  0.0 44.2 %copy-start = (f32[8192]{0:T(1024)S(1)}, f32[8192]{0:T(1024)}, u32[]{:S(2)}) copy-start(f32[8192]{0:T(1024)} %param.15) | copy-start | bytes 98308

commit v4 on v2

--- a/solution.py
+++ b/solution.py
@@ -450,7 +450,7 @@
                 dma((PAIRS, n_head)),
                 dma((PAIRS, n_head)),
             ],
-            compiler_params=pltpu.CompilerParams(collective_id=0, has_side_effects=True),
+            compiler_params=pltpu.CompilerParams(collective_id=0, has_side_effects=True, vmem_limit_bytes=54200 * 1024),
         )(
             b_keys.reshape(tokens, groups // 2, 2, STATE),
             c_queries.reshape(tokens, groups // 2, 2, STATE),

time: 45.9 us -> 47.5 us (1.035)
  local copies, waits for them, and re-layouts: 1.87 us -> 3.86 us
    unnamed x1 -> x9, local copies, waits for them, and re-layouts: 1.87 us -> 3.86 us
where the time goes in v4:
time: 47.5 us; the launch traced here: 47.3 us
  Pallas kernels  43.4 us (91%)
  local copies, waits for them, and re-layouts  3.86 us (8%)
    pallas_call x1, Pallas kernels, body(): pl.pallas_call(run, out_shape=jax.ShapeDtypeStruct((rows, n_head * width)...  43.4 us
    unnamed x9, local copies, waits for them, and re-layouts  3.86 us

profile of v4, /device:TPU:1, one launch (start us, length us, event | category | flops | bytes accessed | tf_op | source)
XLA Modules:
  0.0 47.3 jit_solution(11791518520484896387)
XLA Ops:
  0.0 0.0 copy-start
  0.0 0.9 %copy-done = f32[1024,4,9]{0,1,2:T(4,128)S(1)} copy-done((f32[1024,4,9]{0,1,2:T(4,128)S(1)}, f32[1024,4,9]{0,1,2:T(4,128)}, u32[]{:S(2)}) %copy-start) | copy-done | bytes 147480
  0.9 0.0 copy-start.1
  0.9 0.8 %copy-done.1 = f32[8192]{0:T(1024)S(1)} copy-done((f32[8192]{0:T(1024)S(1)}, f32[8192]{0:T(1024)}, u32[]{:S(2)}) %copy-start.1) | copy-done | bytes 32792
  1.7 0.0 copy-start.2
  1.7 0.7 %copy-done.2 = f32[1024,4]{0,1:T(4,128)S(1)} copy-done((f32[1024,4]{0,1:T(4,128)S(1)}, f32[1024,4]{0,1:T(4,128)}, u32[]{:S(2)}) %copy-start.2) | copy-done | bytes 16408
  2.4 0.0 copy-start.3
  2.4 0.7 %copy-done.3 = s32[256]{0:T(256)S(1)} copy-done((s32[256]{0:T(256)S(1)}, s32[256]{0:T(256)}, u32[]{:S(2)}) %copy-start.3) | copy-done | bytes 1048
  3.1 43.4 %shard_map.82 = bf16[32,8192]{1,0:T(8,128)(2,1)S(1)} custom-call(bf16[1024,4,2,128]{3,2,1,0:T(2,128)(2,1)} %bitcast.8, bf16[1024,4,2,128]{3,2,1,0:T(2,128)(2,1)} %bitcast.9, bf16[1024,256]{1,0:T(8,128)(2,1)} %args_2_.4, bf16[1024,256]{1,0:T(8,128)(2,1)} %args_3_.4, f32[4,1024]{1,0:T(4,128)S(1)} %bitcast.7, f32[9,4,1024]{2,1,0:T(4,128)S(1)} %bitcast.5, ...), custom_call_target="tpu_custom_call" | custom-call | tf_op jit(solution)/shard_map/pallas_call | solution.py:409
  46.5 0.8 %copy.10 = bf16[32,8192]{1,0:T(8,128)(2,1)} copy(bf16[32,8192]{1,0:T(8,128)(2,1)S(1)} %shard_map.82) | data formatting | bytes 1048576
Async XLA Ops:
  0.0 0.9 %copy-start = (f32[1024,4,9]{0,1,2:T(4,128)S(1)}, f32[1024,4,9]{0,1,2:T(4,128)}, u32[]{:S(2)}) copy-start(f32[1024,4,9]{0,1,2:T(4,128)} %param.13) | copy-start | bytes 442372
  0.9 0.8 %copy-start.1 = (f32[8192]{0:T(1024)S(1)}, f32[8192]{0:T(1024)}, u32[]{:S(2)}) copy-start(f32[8192]{0:T(1024)} %param.15) | copy-start | bytes 98308
  1.7 0.7 %copy-start.2 = (f32[1024,4]{0,1:T(4,128)S(1)}, f32[1024,4]{0,1:T(4,128)}, u32[]{:S(2)}) copy-start(f32[1024,4]{0,1:T(4,128)} %param.12) | copy-start | bytes 49156
  2.4 0.7 %copy-start.3 = (s32[256]{0:T(256)S(1)}, s32[256]{0:T(256)}, u32[]{:S(2)}) copy-start(s32[256]{0:T(256)} %args_7_.4) | copy-start | bytes 3076
